TPU v7x, 256 devices: a whole 4x4x8 slice. The times are simulated.
256 devices in a mesh: seq: 64 (over y_lo, z, x), tp: 4 (over y_hi, core).
Axes of the slice: x: 4, y: 4 (y_hi: 2, y_lo: 2; y = y_hi * 2 + y_lo), z: 8, core: 2. Of those that a mesh axis runs over, the one named last changes fastest.
Arguments:
- queries: bfloat16 [16384, 1024], P('seq', 'tp'), may hold values from -6 to 6
- keys: bfloat16 [16384, 1024], P('seq', 'tp'), may hold values from -6 to 6
- values: bfloat16 [16384, 1024], P('seq', 'tp'), may hold values from -6 to 6
- out_weight: bfloat16 [1024, 5120], P('tp'), may hold values from -0.375 to 0.375
- residual: bfloat16 [16384, 5120], P(('seq', 'tp')), may hold values from -3 to 3
- gate: float32 [5120], replicated, may hold values from 0.5 to 1.5
- block_mask: int32 [128, 128], replicated, may hold values from 0 to 1, as said below
Outputs:
- updated: bfloat16 [16384, 5120], P(('seq', 'tp'))
Inputs may be any that keep to these rules, and one draw needn't show every extreme that they name: block_mask[i, j] is 1 wherever |i - j| <= 4. Group the blocks by index of seq, 2 consecutive blocks to an index; where two indices lie more than 2 apart, the rows of one index's query blocks name at most one key block of the other index, and for indices exactly 3 apart this most is always reached.
All inputs are finite; a program needn't handle non-finite values.
Results may differ from a plain program's by a relative error of at most 0.012.
Values may be sent and summed in bfloat16 or wider, within the bound.
A program may use at most 128 MiB of HBM per device.

v0:
```python
import jax
import jax.numpy as jnp
from jax import lax
from jax.sharding import PartitionSpec as P

HD = 128
BLOCK = 128
NEGATIVE = -1e30


def attend(carry, query_heads, key_piece, value_piece, tile_mask, score_scale):
    old_top, old_total, old_summed = carry
    key_rows = key_piece.shape[0]
    query_rows = query_heads.shape[0]
    local_heads = query_heads.shape[1]
    head_size = query_heads.shape[2]
    key_heads = key_piece.reshape(key_rows, local_heads, head_size)
    value_heads = value_piece.reshape(key_rows, local_heads, head_size)
    scores = (
        jnp.einsum("qhd,khd->hqk", query_heads, key_heads, preferred_element_type=jnp.float32)
        * score_scale
    )
    query_tiles = tile_mask.shape[0]
    key_tiles = tile_mask.shape[1]
    allowed = jnp.broadcast_to(
        (tile_mask > 0)[:, None, :, None],
        (query_tiles, query_rows // query_tiles, key_tiles, key_rows // key_tiles),
    )
    allowed = allowed.reshape(query_rows, key_rows)[None, :, :]
    scores = jnp.where(allowed, scores, NEGATIVE)
    new_top = jnp.maximum(old_top, jnp.max(scores, axis=-1))
    weights = jnp.where(allowed, jnp.exp(scores - new_top[:, :, None]), 0.0)
    new_total = jnp.sum(weights, axis=-1)
    added = jnp.einsum(
        "hqk,khd->qhd",
        weights.astype(jnp.bfloat16),
        value_heads,
        preferred_element_type=jnp.float32,
    )
    return (new_top, new_total, added)


def shards(queries, keys, values, out_weight, residual, gate, block_mask):
    tok_rows = queries.shape[0]
    width = queries.shape[1]
    local_heads = width // HD
    my_blocks = tok_rows // BLOCK
    all_blocks = block_mask.shape[0]
    score_scale = 1.0 / HD**0.5
    seq_place = lax.axis_index("seq")
    query_heads = queries.reshape(tok_rows, local_heads, HD)
    start_carry = (
        jnp.full((local_heads, tok_rows), NEGATIVE, jnp.float32),
        jnp.zeros((local_heads, tok_rows), jnp.float32),
        jnp.zeros((tok_rows, local_heads, HD), jnp.float32),
    )
    mask_rows = lax.dynamic_slice(
        block_mask, (seq_place * my_blocks, jnp.int32(0)), (my_blocks, all_blocks)
    )
    key_piece = lax.all_gather(keys, "seq", axis=0, tiled=True)
    value_piece = lax.all_gather(values, "seq", axis=0, tiled=True)
    row_top, totals, summed = attend(
        start_carry, query_heads, key_piece, value_piece, mask_rows, score_scale
    )
    attended = (
        (summed / jnp.transpose(totals)[:, :, None]).reshape(tok_rows, width).astype(jnp.bfloat16)
    )
    branch = lax.psum_scatter(
        jnp.dot(attended, out_weight, preferred_element_type=jnp.float32).astype(jnp.bfloat16),
        "tp",
        scatter_dimension=0,
        tiled=True,
    ).astype(jnp.float32)
    return (residual.astype(jnp.float32) + gate[None, :] * branch).astype(jnp.bfloat16)


def solution(mesh):
    return jax.shard_map(
        shards,
        mesh=mesh,
        in_specs=(
            P("seq", "tp"),
            P("seq", "tp"),
            P("seq", "tp"),
            P("tp", None),
            P(("seq", "tp"), None),
            P(),
            P(),
        ),
        out_specs=P(("seq", "tp"), None),
        check_vma=False,
    )
```

profile of v0, /device:TPU:1, one launch (start us, length us, event | category | flops | bytes accessed | tf_op | source)
XLA Modules:
  0.0 676.6 jit_solution(8116730190612022189)
XLA Ops:
  6.5 0.0 copy-start
  6.5 0.0 copy-start.3
  6.5 0.0 all-gather.3.cloned.1.call-start
  6.5 1.8 copy.10
  8.4 0.0 all-gather.3.cloned.1.call-update
  8.4 0.0 all-gather.5.cloned.1.call-start
  8.4 0.7 all-gather.5.cloned.1.call-update
  9.1 0.0 reduce-scatter.2.cloned.1.call-start
  9.2 0.7 dynamic-slice_compare_fusion
  9.9 2.2 broadcast_in_dim.32
  12.1 19.1 %copy.24 = pred[32,8,128,128]{3,1,2,0:T(8,128)(4,1)} copy(pred[32,8,128,128]{3,2,1,0:T(8,128)(4,1)S(1)} %bitcast.31) | data formatting | bytes 8388608
  31.2 211.7 %all-gather.3.cloned.1.call-done = bf16[16384,256]{0,1:T(8,128)(2,1)} async-done(((bf16[256,256]{0,1:T(8,128)(2,1)}), bf16[16384,256]{0,1:T(8,128)(2,1)}) %all-gather.3.cloned.1.call-update) | async-done | bytes 8388624 | tf_op jit(solution)/shard_map/all_gather | solution.py:60
  242.9 0.0 copy-done.3
  242.9 19.4 %fusion = (f32[2,256]{1,0:T(2,128)S(1)}, f32[2,256,16384]{2,1,0:T(8,128)}) fusion(pred[256,16384]{1,0:T(8,128)(4,1)} %bitcast.28, bf16[16384,2,128]{0,2,1:T(8,128)(2,1)} %bitcast.35, bf16[256,256]{1,0:T(8,128)(2,1)S(1)} %copy-done.3), kind=kOutput, calls=%fused_computation.2 | convolution fusion | flops 2172648960 | bytes 46270464 | tf_op jit(solution)/shard_map/qhd,khd->hqk/dot_general | solution.py:20
  262.3 16.3 %fusion.1 = f32[2,256]{1,0:T(2,128)S(1)} fusion(f32[2,256,16384]{2,1,0:T(8,128)} %get-tuple-element.6, f32[2,256]{1,0:T(2,128)S(1)} %broadcast_maximum_fusion, pred[256,16384]{1,0:T(8,128)(4,1)} %bitcast.29), kind=kLoop, calls=%fused_computation.3 | loop fusion | flops 41942528 | bytes 37752832 | tf_op jit(solution)/shard_map/reduce_sum | solution.py:33
  278.6 273.0 %all-gather.5.cloned.1.call-done = bf16[16384,256]{1,0:T(8,128)(2,1)} async-done(((bf16[256,256]{1,0:T(8,128)(2,1)}), bf16[16384,256]{1,0:T(8,128)(2,1)}) %all-gather.5.cloned.1.call-update) | async-done | bytes 8388624 | tf_op jit(solution)/shard_map/all_gather | solution.py:61
  551.6 11.9 %copy.13 = bf16[16384,256]{0,1:T(8,128)(2,1)} copy(bf16[16384,256]{1,0:T(8,128)(2,1)} %all-gather.5.cloned.1.call-done) | data formatting | bytes 16777216 | tf_op jit(solution)/shard_map/all_gather | solution.py:61
  563.5 0.0 copy-start.2
  563.5 17.3 %fusion.12 = bf16[256,2,128]{0,2,1:T(8,128)(2,1)S(1)} fusion(bf16[16384,2,128]{0,2,1:T(8,128)(2,1)} %bitcast.32, f32[2,256,16384]{2,1,0:T(8,128)} %get-tuple-element.6, f32[2,256]{1,0:T(2,128)S(1)} %broadcast_maximum_fusion, pred[256,16384]{1,0:T(8,128)(4,1)} %bitcast.30, f32[256,2]{0,1:T(2,128)S(1)} %bitcast.34), kind=kOutput, calls=%fused_computation.12 | convolution fusion | flops 2189557760 | bytes 46272512 | tf_op jit(solution)/shard_map/hqk,khd->qhd/dot_general | solution.py:34
  580.9 0.0 copy-start.1
  580.9 0.0 copy-done
  580.9 2.4 convolution_convert_fusion
  583.3 0.0 reduce-scatter.2.cloned.1.call-update
  583.3 84.6 %reduce-scatter.2.cloned.1.call-done = bf16[64,5120]{1,0:T(8,128)(2,1)} async-done(((bf16[256,5120]{1,0:T(8,128)(2,1)}), bf16[64,5120]{1,0:T(8,128)(2,1)}) %reduce-scatter.2.cloned.1.call-update) | async-done | bytes 655376 | tf_op jit(solution)/shard_map/reduce_scatter | solution.py:68
  667.9 0.0 copy-done.2
  667.9 0.0 copy-done.1
  667.9 2.1 add_convert_fusion
  (1 shorter events, 0.0 us)
Async XLA Ops:
  6.5 574.3 %copy-start = (bf16[256,5120]{1,0:T(8,128)(2,1)S(1)}, bf16[256,5120]{1,0:T(8,128)(2,1)}, u32[]{:S(2)}) copy-start(bf16[256,5120]{1,0:T(8,128)(2,1)} %param.10) | copy-start | bytes 7864324
  6.5 236.4 %copy-start.3 = (bf16[256,256]{1,0:T(8,128)(2,1)S(1)}, bf16[256,256]{1,0:T(8,128)(2,1)}, u32[]{:S(2)}) copy-start(bf16[256,256]{1,0:T(8,128)(2,1)} %param.7) | copy-start | bytes 393220
  6.5 236.4 %all-gather.3.cloned.1.call-start = ((), (), s32[]{:S(2)}) async-start(), calls=%async_computation.1 | async-start | bytes 8519680 | tf_op jit(solution)/shard_map/all_gather | solution.py:60
  8.4 543.2 %all-gather.5.cloned.1.call-start = ((), (), s32[]{:S(2)}) async-start(), calls=%async_computation.2 | async-start | bytes 8519680 | tf_op jit(solution)/shard_map/all_gather | solution.py:61
  9.1 658.8 %reduce-scatter.2.cloned.1.call-start = ((), (), s32[]{:S(2)}) async-start(), calls=%async_computation.3 | async-start | bytes 3276800 | tf_op jit(solution)/shard_map/reduce_scatter | solution.py:68
  563.5 104.4 %copy-start.2 = (f32[5120]{0:T(1024)S(1)}, f32[5120]{0:T(1024)}, u32[]{:S(2)}) copy-start(f32[5120]{0:T(1024)} %param.12) | copy-start | bytes 61444
  580.9 87.1 %copy-start.1 = (bf16[64,5120]{1,0:T(8,128)(2,1)S(1)}, bf16[64,5120]{1,0:T(8,128)(2,1)}, u32[]{:S(2)}) copy-start(bf16[64,5120]{1,0:T(8,128)(2,1)} %param.11) | copy-start | bytes 1966084
Sparse Core Ops, SparseCore 0:
  9.0 233.7 all-gather.2
  244.7 306.9 all-gather.4
  583.4 84.4 reduce-scatter.1
where the time goes:
time: 677 us
  waiting for transfers between devices  570 us (84%)
  matrix products  39.1 us (6%)
  local copies, waits for them, and re-layouts  35 us (5%)
  other arithmetic  19.1 us (3%)
  between operations  13.1 us (2%)
    all_gather x1, waiting for transfers between devices, shards(): value_piece = lax.all_gather(values, 'seq', axis=0, tiled=True)  273 us
    all_gather x1, waiting for transfers between devices, shards(): key_piece = lax.all_gather(keys, 'seq', axis=0, tiled=True)  212 us
    reduce_scatter x1, waiting for transfers between devices, shards(): lax.psum_scatter(jnp.dot(attended, out_weight, preferred_element_type=jnp...  84.6 us
    unnamed x10, local copies, waits for them, and re-layouts  21 us
    dot_general x1, matrix products, attend(): jnp.einsum('qhd,khd->hqk', query_heads, key_heads, preferred_element_type...  19.4 us
    dot_general x1, matrix products, attend(): jnp.einsum('hqk,khd->qhd', weights.astype(jnp.bfloat16), value_heads, pre...  17.3 us
    reduce_sum x1, other arithmetic, attend(): new_total = jnp.sum(weights, axis=-1)  16.3 us
  transfers between devices with their start and end apart: 3, of which 3 were waited for; matrix products, arithmetic and copies ran while one was open for 9% of the time, Pallas kernels for 0%

commit v1 on v0

--- a/solution.py
+++ b/solution.py
@@ -57,8 +57,11 @@
     mask_rows = lax.dynamic_slice(
         block_mask, (seq_place * my_blocks, jnp.int32(0)), (my_blocks, all_blocks)
     )
-    key_piece = lax.all_gather(keys, "seq", axis=0, tiled=True)
-    value_piece = lax.all_gather(values, "seq", axis=0, tiled=True)
+    key_piece, value_piece = jnp.split(
+        lax.all_gather(jnp.concatenate([keys, values], axis=1), "seq", axis=0, tiled=True),
+        [keys.shape[1]],
+        axis=1,
+    )
     row_top, totals, summed = attend(
         start_carry, query_heads, key_piece, value_piece, mask_rows, score_scale
     )

time: 677 us -> 468 us (0.69)
  waiting for transfers between devices: 570 us -> 355 us
  local copies, waits for them, and re-layouts: 35 us -> 45.6 us
    all_gather x2 -> x1, waiting for transfers between devices: 485 us -> 261 us  [shards(): lax.all_gather(jnp.concatenate([keys, values], axis=1), 'seq', axis=0, ti...]
    all_gather x1 -> x0, local copies, waits for them, and re-layouts: 11.9 us -> none  [shards(): value_piece = lax.all_gather(values, 'seq', axis=0, tiled=True)]
    split x0 -> x1, local copies, waits for them, and re-layouts: none -> 11.8 us  [shards(): jnp.split(lax.all_gather(jnp.concatenate([keys, values], axis=1), 'seq',...]
    broadcast_in_dim x0 -> x1, local copies, waits for them, and re-layouts: none -> 10.4 us  [attend(): weights = jnp.where(allowed, jnp.exp(scores - new_top[:, :, None]), 0.0)]
    reduce_scatter x1, waiting for transfers between devices: 84.6 us -> 93.2 us  [shards(): lax.psum_scatter(jnp.dot(attended, out_weight, preferred_element_type=jnp...]
    unnamed x10 -> x13, local copies, waits for them, and re-layouts: 21 us -> 21.2 us
  transfers between devices with their start and end apart: 3 -> 2, of which waited for: 3 -> 2; matrix products, arithmetic and copies ran while one was open for 9% -> 7% of each run, Pallas kernels for 0% -> 0%
where the time goes in v1:
time: 468 us
  waiting for transfers between devices  355 us (76%)
  local copies, waits for them, and re-layouts  45.6 us (10%)
  matrix products  35.3 us (8%)
  other arithmetic  18.8 us (4%)
  between operations  13.5 us (3%)
    all_gather x1, waiting for transfers between devices, shards(): lax.all_gather(jnp.concatenate([keys, values], axis=1), 'seq', axis=0, ti...  261 us
    reduce_scatter x1, waiting for transfers between devices, shards(): lax.psum_scatter(jnp.dot(attended, out_weight, preferred_element_type=jnp...  93.2 us
    unnamed x13, local copies, waits for them, and re-layouts  21.2 us
    dot_general x1, matrix products, attend(): jnp.einsum('hqk,khd->qhd', weights.astype(jnp.bfloat16), value_heads, pre...  17 us
    dot_general x1, matrix products, attend(): jnp.einsum('qhd,khd->hqk', query_heads, key_heads, preferred_element_type...  16 us
    reduce_sum x1, other arithmetic, attend(): new_total = jnp.sum(weights, axis=-1)  15.2 us
    split x1, local copies, waits for them, and re-layouts, shards(): jnp.split(lax.all_gather(jnp.concatenate([keys, values], axis=1), 'seq',...  11.8 us
    broadcast_in_dim x1, local copies, waits for them, and re-layouts, attend(): weights = jnp.where(allowed, jnp.exp(scores - new_top[:, :, None]), 0.0)  10.4 us
  transfers between devices with their start and end apart: 2, of which 2 were waited for; matrix products, arithmetic and copies ran while one was open for 7% of the time, Pallas kernels for 0%

profile of v1, /device:TPU:1, one launch (start us, length us, event | category | flops | bytes accessed | tf_op | source)
XLA Modules:
  0.0 467.8 jit_solution(6994037452535211246)
XLA Ops:
  6.5 0.0 copy-start
  6.5 0.0 all-gather.2.cloned.1.call-start
  6.5 1.2 copy.12
  7.7 1.0 copy.13
  8.7 0.7 pad_maximum_fusion
  9.4 0.0 all-gather.2.cloned.1.call-update
  9.5 0.0 reduce-scatter.2.cloned.1.call-start
  9.5 0.7 dynamic-slice_compare_fusion
  10.2 2.2 broadcast_in_dim.32
  12.4 19.0 %copy.29 = pred[32,8,128,128]{3,1,2,0:T(8,128)(4,1)} copy(pred[32,8,128,128]{3,2,1,0:T(8,128)(4,1)S(1)} %bitcast.45) | data formatting | bytes 8388608
  31.4 10.4 %copy.14 = pred[256,16384]{0,1:T(8,128)(4,1)} copy(pred[256,16384]{1,0:T(8,128)(4,1)} %bitcast.46) | data formatting | bytes 8388608 | tf_op jit(solution)/shard_map/jit(_where)/broadcast_in_dim | solution.py:32
  41.8 0.0 copy-start.4
  41.8 261.4 %all-gather.2.cloned.1.call-done = bf16[16384,512]{0,1:T(8,128)(2,1)} async-done(((bf16[256,512]{0,1:T(8,128)(2,1)}), bf16[16384,512]{0,1:T(8,128)(2,1)}) %all-gather.2.cloned.1.call-update) | async-done | bytes 16777232 | tf_op jit(solution)/shard_map/all_gather | solution.py:61
  303.2 0.0 copy-start.1
  303.2 11.8 %fusion.21 = (bf16[16384,256]{0,1:T(8,128)(2,1)}, bf16[16384,256]{0,1:T(8,128)(2,1)}) fusion(bf16[16384,512]{0,1:T(8,128)(2,1)} %all-gather.2.cloned.1.call-done), kind=kLoop, calls=%fused_computation.22 | loop fusion | bytes 33554432 | tf_op jit(solution)/shard_map/split | solution.py:60
  315.0 0.0 copy-done.4
  315.0 0.0 copy-done.1
  315.0 16.0 %fusion = (f32[2,256]{1,0:T(2,128)S(1)}, f32[2,16384,256]{2,1,0:T(8,128)}) fusion(pred[256,16384]{0,1:T(8,128)(4,1)S(1)} %copy-done.1, bf16[16384,2,128]{0,2,1:T(8,128)(2,1)} %bitcast.48, bf16[256,256]{1,0:T(8,128)(2,1)S(1)} %copy-done.4), kind=kOutput, calls=%fused_computation.2 | convolution fusion | flops 2172648960 | bytes 46270464 | tf_op jit(solution)/shard_map/qhd,khd->hqk/dot_general | solution.py:20
  331.0 15.2 %fusion.1 = f32[2,256]{1,0:T(2,128)S(1)} fusion(f32[2,16384,256]{2,1,0:T(8,128)} %get-tuple-element.8, f32[2,256]{1,0:T(2,128)S(1)} %broadcast_maximum_fusion, pred[256,16384]{0,1:T(8,128)(4,1)S(1)} %copy-done.1), kind=kLoop, calls=%fused_computation.3 | loop fusion | flops 41942528 | bytes 37752832 | tf_op jit(solution)/shard_map/reduce_sum | solution.py:33
  346.3 0.0 copy-start.3
  346.3 17.0 %fusion.12 = bf16[256,2,128]{0,2,1:T(8,128)(2,1)S(1)} fusion(bf16[16384,2,128]{0,2,1:T(8,128)(2,1)} %bitcast.47, f32[2,16384,256]{2,1,0:T(8,128)} %get-tuple-element.8, f32[2,256]{1,0:T(2,128)S(1)} %broadcast_maximum_fusion, pred[256,16384]{0,1:T(8,128)(4,1)S(1)} %copy-done.1, f32[256,2]{0,1:T(2,128)S(1)} %bitcast.50), kind=kOutput, calls=%fused_computation.12 | convolution fusion | flops 2189557760 | bytes 46272512 | tf_op jit(solution)/shard_map/hqk,khd->qhd/dot_general | solution.py:34
  363.3 0.0 copy-start.2
  363.3 0.0 copy-done
  363.3 2.4 convolution_convert_fusion
  365.7 0.0 reduce-scatter.2.cloned.1.call-update
  365.7 93.2 %reduce-scatter.2.cloned.1.call-done = bf16[64,5120]{1,0:T(8,128)(2,1)} async-done(((bf16[256,5120]{1,0:T(8,128)(2,1)}), bf16[64,5120]{1,0:T(8,128)(2,1)}) %reduce-scatter.2.cloned.1.call-update) | async-done | bytes 655376 | tf_op jit(solution)/shard_map/reduce_scatter | solution.py:71
  458.8 0.0 copy-done.3
  458.9 0.0 copy-done.2
  458.9 2.1 add_convert_fusion
  (1 shorter events, 0.0 us)
Async XLA Ops:
  6.5 356.7 %copy-start = (bf16[256,5120]{1,0:T(8,128)(2,1)S(1)}, bf16[256,5120]{1,0:T(8,128)(2,1)}, u32[]{:S(2)}) copy-start(bf16[256,5120]{1,0:T(8,128)(2,1)} %param.10) | copy-start | bytes 7864324
  6.5 296.7 %all-gather.2.cloned.1.call-start = ((), (), s32[]{:S(2)}) async-start(), calls=%async_computation.1 | async-start | bytes 17039360 | tf_op jit(solution)/shard_map/all_gather | solution.py:61
  9.5 449.4 %reduce-scatter.2.cloned.1.call-start = ((), (), s32[]{:S(2)}) async-start(), calls=%async_computation.2 | async-start | bytes 3276800 | tf_op jit(solution)/shard_map/reduce_scatter | solution.py:71
  41.8 273.2 %copy-start.4 = (bf16[256,256]{1,0:T(8,128)(2,1)S(1)}, bf16[256,256]{1,0:T(8,128)(2,1)}, u32[]{:S(2)}) copy-start(bf16[256,256]{1,0:T(8,128)(2,1)} %param.7) | copy-start | bytes 393220
  303.2 11.8 %copy-start.1 = (pred[256,16384]{0,1:T(8,128)(4,1)S(1)}, pred[256,16384]{0,1:T(8,128)(4,1)}, u32[]{:S(2)}) copy-start(pred[256,16384]{0,1:T(8,128)(4,1)} %copy.14) | copy-start | bytes 12582916
  346.3 112.6 %copy-start.3 = (f32[5120]{0:T(1024)S(1)}, f32[5120]{0:T(1024)}, u32[]{:S(2)}) copy-start(f32[5120]{0:T(1024)} %param.12) | copy-start | bytes 61444
  363.3 95.6 %copy-start.2 = (bf16[64,5120]{1,0:T(8,128)(2,1)S(1)}, bf16[64,5120]{1,0:T(8,128)(2,1)}, u32[]{:S(2)}) copy-start(bf16[64,5120]{1,0:T(8,128)(2,1)} %param.11) | copy-start | bytes 1966084
Sparse Core Ops, SparseCore 0:
  9.6 293.5 all-gather.1
  365.8 93.0 reduce-scatter.1
